TPU v7x, 32 devices: a whole 2x2x4 slice. The times are simulated.
32 devices in a mesh: seg: 8 (over z, x), sub: 4 (over y, core).
Axes of the slice: x: 2, y: 2, z: 4, core: 2. Of those that a mesh axis runs over, the one named last changes fastest.
Arguments:
- leaf_mult: float32 [32768, 256], P(('seg', 'sub')), may hold values from -6 to 6
- m2m_ops: float32 [8, 256, 256], replicated, may hold values from -0.125 to 0.125
- m2l_ops: float32 [32, 256, 256], replicated, may hold values from -0.0625 to 0.0625
- owner_box: int32 [4096], P(('seg', 'sub')), may hold values from 0 to 4095, as said below
- src_list: int32 [4096, 32], P(('seg', 'sub')), may hold values from -1 to 4095, as said below
Outputs:
- parent_mult: float32 [4096, 256], P(('seg', 'sub'))
- owned_mult: float32 [4096, 256], P(('seg', 'sub'))
- local_exp: float32 [4096, 256], P(('seg', 'sub'))
Inputs may be any that keep to these rules, and one draw needn't show every extreme that they name: `owner_box`: each aligned block of 512 rows, the g-th, holds every box id from g * 512 to (g + 1) * 512 - 1 once. `src_list`: A slot of a row in the g-th aligned block of 512 rows is -1 or names a box of the blocks g - 1, g or g + 1 of Morton order, each block being 512 consecutive ids.
All inputs are finite; a program needn't handle non-finite values.
Results may differ from a plain program's by a relative error of at most 0.000082.
Values sent between devices are 32-bit elements; how exact they have to be, the bound alone decides.
A program may use at most 64 MiB of HBM per device.

v0:
```python
import functools

import jax
import jax.numpy as jnp
from jax import lax
from jax.experimental import pallas as pl
from jax.experimental.pallas import tpu as pltpu
from jax.sharding import PartitionSpec as P

MESH = pl.DeviceIdType.MESH
LANES = 128
BATCH = 16
PARTS = 4


def split(value):
    high = value.astype(jnp.bfloat16)
    low = (value - high.astype(jnp.float32)).astype(jnp.bfloat16)
    return high, low


def kernel(
    n_seg, n_sub, leaf_hbm, up_hbm, src_t, owner, ops_hbm, sums,
    leaf, up, parent,
    pair, far, pair_parts, far_parts, ops, ops_high, ops_low, index, picked,
    ops_sem, leaf_sem, up_sem, send_sem, recv_sem,
):
    seg, sub = lax.axis_index("seg"), lax.axis_index("sub")
    rows, width = parent.shape
    slots = src_t.shape[0]
    n_high = n_sub // 2
    side, core, high = seg % 2, sub % 2, sub // 2
    partner = seg + 1 - 2 * side
    other_side = 1 - side
    sibling = sub + 1 - 2 * core
    target = seg + 2 - 4 * side
    origin = seg - 2 + 4 * side
    has_target = (target >= 0) & (target < n_seg)
    has_origin = (origin >= 0) & (origin < n_seg)
    half = rows // PARTS
    group_rows = rows * n_sub

    n_up = up.shape[0]
    leaf_copies = [
        pltpu.make_async_copy(leaf_hbm.at[:, pl.ds(t * LANES, LANES)], leaf.at[t], leaf_sem.at[t])
        for t in range(width // LANES)
    ]
    for c in leaf_copies:
        c.start()
    up_copies = [pltpu.make_async_copy(up_hbm.at[c], up.at[c], up_sem.at[c]) for c in range(n_up)]
    for c in up_copies:
        c.start()
    middle = slots // 2
    ops_copies = [
        pltpu.make_async_copy(ops_hbm.at[at], ops.at[at], ops_sem.at[k])
        for k, at in enumerate((pl.ds(0, middle), pl.ds(middle, slots - middle)))
    ]

    barrier = pltpu.get_barrier_semaphore()

    def greet(to_seg, to_sub):
        pl.semaphore_signal(barrier, inc=1, device_id=(to_seg, to_sub), device_id_type=MESH)

    def peer(step):
        return lax.rem(high + step, n_high) * 2 + core

    greet(seg, sibling)
    greet(partner, sub)
    for step in range(1, n_high):
        greet(seg, peer(step))

    @pl.when(has_target)
    def _():
        greet(target, sub)

    @pl.when(has_origin)
    def _():
        greet(origin, sub)

    pad = jnp.full((LANES - slots - 8, rows), -1, jnp.int32)
    table = jnp.concatenate([src_t[...], jnp.broadcast_to(owner[...], (8, rows)), pad], axis=0)
    pair_start = (seg - side) * group_rows
    table = jnp.where(table < 0, -(1 << 28), table - pair_start)
    table = table.T
    for j in range(slots + 1):
        index[j] = jnp.broadcast_to(table[:, j : j + 1], (rows, LANES))

    def three_products(first, second, ops_first, ops_second):
        both = jnp.concatenate([first, second], axis=0)
        out = jnp.dot(both, ops_first, preferred_element_type=jnp.float32)
        return out[:rows] + out[rows:] + jnp.dot(first, ops_second, preferred_element_type=jnp.float32)

    for c in leaf_copies:
        c.wait()
    total = jnp.zeros((rows, width), jnp.float32)
    for c in range(n_up):
        up_copies[c].wait()
        if c == n_up // 2:
            for one in ops_copies:
                one.start()
        child = jnp.concatenate(
            [leaf[t, pl.ds(c, rows, stride=n_up), :] for t in range(width // LANES)], axis=1
        )
        total = total + three_products(*split(child), *split(up[c]))
    parent[...] = total

    pl.semaphore_wait(barrier, 1 + n_high + has_target.astype(jnp.int32) + has_origin.astype(jnp.int32))

    names = {}

    def copy(name, src, dst, to_seg, to_sub):
        k = names.setdefault(name, len(names))
        return pltpu.make_async_remote_copy(
            src_ref=src, dst_ref=dst, send_sem=send_sem.at[k], recv_sem=recv_sem.at[k],
            device_id=(to_seg, to_sub), device_id_type=MESH,
        )

    def piece(part):
        return pl.ds(part * half, half)

    sent = []

    def go(c):
        c.start()
        sent.append(c)
        return c

    def to_x(part):
        return copy(("x", part), parent.at[piece(part)], pair.at[side, sub, piece(part)], partner, sub)

    def from_x(part):
        return copy(("x", part), parent.at[piece(part)], pair.at[other_side, sub, piece(part)], partner, sub)

    def to_y(step, part):
        return copy(("y", step, part), parent.at[piece(part)], pair.at[side, sub, piece(part)], seg, peer(step))

    def from_y(step, part):
        at = pair.at[side, peer(n_high - step), piece(part)]
        return copy(("y", step, part), parent.at[piece(part)], at, seg, peer(step))

    def xy(step, part):
        at = pair.at[other_side, sub, piece(part)]
        return copy(("xy", step, part), at, at, seg, peer(step))

    def from_xy(step, part):
        at = pair.at[other_side, peer(n_high - step), piece(part)]
        return copy(("xy", step, part), at, at, seg, peer(step))

    def yx(step, part):
        at = pair.at[side, peer(step), piece(part)]
        return copy(("yx", step, part), at, at, partner, sub)

    def from_yx(step, part):
        at = pair.at[other_side, peer(step), piece(part)]
        return copy(("yx", step, part), at, at, partner, sub)

    def z(step, part):
        return copy(
            ("z", step, part), pair.at[other_side, peer(step), piece(part)],
            far.at[peer(step), piece(part)], target, sub,
        )

    def to_sibling(step, which):
        at = far.at[peer(step)] if which == 2 else pair.at[(side, other_side)[which], peer(step)]
        src = parent if (step, which) == (0, 0) else at
        return copy(("s", step, which), src, at, seg, sibling)

    def from_sibling(step, which):
        s = lax.rem(high + step, n_high) * 2 + 1 - core
        at = far.at[s] if which == 2 else pair.at[(side, other_side)[which], s]
        return copy(("s", step, which), at, at, seg, sibling)

    for part in range(PARTS):
        go(to_x(part))
        for step in range(1, n_high):
            go(to_y(step, PARTS - 1 - part))
    go(to_sibling(0, 0))
    pair[side, sub] = parent[...]
    sums[0] = parent[...]

    def split_ops(start, stop):
        @pl.loop(start, stop)
        def _(j):
            ops_high[j], ops_low[j] = split(ops[j])

    ops_copies[0].wait()
    split_ops(0, middle)

    for part in range(PARTS):
        from_x(part).wait_recv()

        @pl.when(has_target)
        def _():
            z(0, part).start()

        for step in range(1, n_high):
            if part < PARTS // 2:
                go(xy(step, part))
        for step in range(1, n_high):
            from_y(step, PARTS - 1 - part).wait_recv()
            if part < PARTS // 2:
                go(yx(n_high - step, PARTS - 1 - part))

    go(to_sibling(0, 1))
    for step in range(1, n_high):
        go(to_sibling(n_high - step, 0))

    for part in range(PARTS // 2):
        for step in range(1, n_high):
            from_xy(step, part).wait_recv()

            @pl.when(has_target)
            def _():
                z(n_high - step, part).start()

            from_yx(step, PARTS - 1 - part).wait_recv()

            @pl.when(has_target)
            def _():
                z(step, PARTS - 1 - part).start()

    for step in range(1, n_high):
        go(to_sibling(step, 1))

    ops_copies[1].wait()
    split_ops(middle, slots)

    for step in range(n_high):
        from_sibling(step, 0).wait_recv()
    for step in range(n_high):
        from_sibling(step, 1).wait_recv()

    lane = lax.broadcasted_iota(jnp.int32, (1, LANES), 1)

    def one_hot(chosen, count, base):
        tiles = []
        for t in range(count // LANES):
            hit = chosen == lane + (base + t * LANES)
            tiles.append(jnp.where(hit, 1.0, 0.0).astype(jnp.bfloat16))
        return jnp.concatenate(tiles, axis=1)

    for s in range(2):
        for k in range(n_sub):
            at = pl.ds((s * n_sub + k) * rows, rows)
            pair_parts[at, :width], pair_parts[at, width:] = split(pair[s, k])

    chosen = index[slots]
    own_rows = pair_parts[pl.ds(pl.multiple_of(side * group_rows, LANES), group_rows), :]
    got = jnp.dot(one_hot(chosen, group_rows, side * group_rows), own_rows, preferred_element_type=jnp.float32)
    sums[1] = got[:, :width]
    sums[2] = got[:, width:]

    def near(start, stop):
        @pl.loop(start, stop)
        def _(b):
            chosen = index[pl.ds(b * BATCH, BATCH)].reshape(BATCH * rows, LANES)
            got = jnp.dot(
                one_hot(chosen, 2 * group_rows, 0), pair_parts[...], preferred_element_type=jnp.float32
            )
            picked[b] = got.astype(jnp.bfloat16)

    batches = slots // BATCH
    near(0, batches // 2)

    @pl.when(has_origin)
    def _():
        for step in range(n_high):
            for part in range(PARTS):
                z(step, part).wait_recv()
            to_sibling(step, 2).start()

    near(batches // 2, batches)

    @pl.when(has_origin)
    def _():
        for step in range(n_high):
            from_sibling(step, 2).wait_recv()
        for k in range(n_sub):
            at = pl.ds(k * rows, rows)
            far_parts[at, :width], far_parts[at, width:] = split(far[k])

    far_base = -group_rows + side * (3 * group_rows)
    sums[3] = jnp.zeros((rows, width), jnp.float32)
    sums[4] = jnp.zeros((rows, width), jnp.float32)

    def translate(with_far):
        @pl.loop(0, batches)
        def _(b):
            got = picked[b]
            if with_far:
                chosen = index[pl.ds(b * BATCH, BATCH)].reshape(BATCH * rows, LANES)
                more = jnp.dot(
                    one_hot(chosen, group_rows, far_base), far_parts[...], preferred_element_type=jnp.float32
                )
                got = got + more.astype(jnp.bfloat16)
            total, rest = sums[3], sums[4]
            for i in range(BATCH):
                mine = got[i * rows : (i + 1) * rows]
                first, second = mine[:, :width], mine[:, width:]
                both = jnp.concatenate([first, second], axis=0)
                out = jnp.dot(both, ops_high[b * BATCH + i], preferred_element_type=jnp.float32)
                total = total + out[:rows]
                rest = rest + out[rows:]
                rest = rest + jnp.dot(first, ops_low[b * BATCH + i], preferred_element_type=jnp.float32)
            sums[3], sums[4] = total, rest

    @pl.when(has_origin)
    def _():
        translate(True)

    @pl.when(jnp.logical_not(has_origin))
    def _():
        translate(False)

    for c in sent:
        c.wait_send()

    @pl.when(has_target)
    def _():
        for step in range(n_high):
            for part in range(PARTS):
                z(step, part).wait_send()

    @pl.when(has_origin)
    def _():
        for step in range(n_high):
            to_sibling(step, 2).wait_send()


def on_device(n_seg, n_sub, leaf_mult, m2m_ops, m2l_ops, owner_box, src_list):
    rows, width = leaf_mult.shape[0] // 8, leaf_mult.shape[1]
    slots = src_list.shape[1]
    n_high = n_sub // 2
    messages = PARTS * (3 * n_high - 1) + 3 * n_high
    group_rows = rows * n_sub
    vmem = pl.BlockSpec(memory_space=pltpu.VMEM)
    hbm = pl.BlockSpec(memory_space=pl.ANY)
    half_type = jnp.bfloat16
    sums = pl.pallas_call(
        functools.partial(kernel, n_seg, n_sub),
        out_shape=jax.ShapeDtypeStruct((5, rows, width), jnp.float32),
        in_specs=[hbm, hbm, vmem, vmem, hbm],
        out_specs=vmem,
        scratch_shapes=[
            pltpu.VMEM((width // LANES, leaf_mult.shape[0], LANES), jnp.float32),
            pltpu.VMEM(m2m_ops.shape, jnp.float32),
            pltpu.VMEM((rows, width), jnp.float32),
            pltpu.VMEM((2, n_sub, rows, width), jnp.float32),
            pltpu.VMEM((n_sub, rows, width), jnp.float32),
            pltpu.VMEM((2 * group_rows, 2 * width), half_type),
            pltpu.VMEM((group_rows, 2 * width), half_type),
            pltpu.VMEM(m2l_ops.shape, jnp.float32),
            pltpu.VMEM(m2l_ops.shape, half_type),
            pltpu.VMEM(m2l_ops.shape, half_type),
            pltpu.VMEM((slots + 1, rows, LANES), jnp.int32),
            pltpu.VMEM((slots // BATCH, BATCH * rows, 2 * width), half_type),
            pltpu.SemaphoreType.DMA((2,)),
            pltpu.SemaphoreType.DMA((width // LANES,)),
            pltpu.SemaphoreType.DMA((m2m_ops.shape[0],)),
            pltpu.SemaphoreType.DMA((messages,)),
            pltpu.SemaphoreType.DMA((messages,)),
        ],
        compiler_params=pltpu.CompilerParams(
            collective_id=0, has_side_effects=True, vmem_limit_bytes=60 << 20
        ),
    )(leaf_mult, m2m_ops, src_list.T, owner_box.reshape(1, rows), m2l_ops)
    return (sums[0], sums[1] + sums[2], sums[3] + sums[4])


def solution(mesh):
    n_seg, n_sub = mesh.shape["seg"], mesh.shape["sub"]
    in_specs = (P(("seg", "sub"), None), P(), P(), P(("seg", "sub")), P(("seg", "sub"), None))
    out_specs = (P(("seg", "sub"), None), P(("seg", "sub"), None), P(("seg", "sub"), None))
    return jax.shard_map(
        functools.partial(on_device, n_seg, n_sub),
        mesh=mesh, in_specs=in_specs, out_specs=out_specs, check_vma=False,
    )
```

profile of v0, /device:TPU:17, one launch (start us, length us, event | category | flops | bytes accessed | tf_op | source)
XLA Modules:
  0.0 29.0 jit_solution(9053500842075132052)
XLA Ops:
  0.6 26.4 %shard_map.76 = f32[5,128,256]{2,1,0:T(8,128)} custom-call(f32[1024,256]{1,0:T(8,128)} %leaf_hbm.1, f32[8,256,256]{2,1,0:T(8,128)} %up_hbm.1, s32[32,128]{1,0:T(8,128)} %bitcast.8, s32[1,128]{1,0:T(1,128)} %bitcast.9, f32[32,256,256]{2,1,0:T(8,128)} %ops_hbm.1), custom_call_target="tpu_custom_call" | custom-call | tf_op jit(solution)/shard_map/pallas_call | solution.py:339
  27.0 1.9 %add_bitcast_fusion = (f32[128,256]{1,0:T(8,128)}, f32[128,256]{1,0:T(8,128)}, f32[128,256]{1,0:T(8,128)}) fusion(f32[5,128,256]{2,1,0:T(8,128)} %shard_map.76), kind=kLoop, calls=%fused_computation | loop fusion | flops 65536 | bytes 1048576 | tf_op jit(solution)/shard_map/add | solution.py:367
where the time goes:
time: 29.2 us; the launch traced here: 29 us
  Pallas kernels  26.4 us (90%)
  other arithmetic  1.92 us (7%)
  between operations  0.64 us (2%)
    pallas_call x1, Pallas kernels, on_device(): pl.pallas_call(functools.partial(kernel, n_seg, n_sub), out_shape=jax.Sha...  26.4 us
    add x1, other arithmetic, on_device(): return (sums[0], sums[1] + sums[2], sums[3] + sums[4])  1.92 us

commit v1 on v0

v1 whole, which is shorter than its diff:
```python
import functools

import jax
import jax.numpy as jnp
from jax import lax
from jax.experimental import pallas as pl
from jax.experimental.pallas import tpu as pltpu
from jax.sharding import PartitionSpec as P

MESH = pl.DeviceIdType.MESH
LANES = 128
BATCH = 4
PARTS = 4
EXCHANGE_VMEM = 24 << 20
COMBINE_VMEM = 16 << 20


def split(value):
    high = value.astype(jnp.bfloat16)
    low = (value - high.astype(jnp.float32)).astype(jnp.bfloat16)
    return high, low


def exchange(
    n_seg, n_sub, leaf_hbm, up_hbm, ops_hbm, box, ops_high, ops_low,
    leaf, up, ops, ops_sem, leaf_sem, up_sem, send_sem, recv_sem,
):
    seg, sub = lax.axis_index("seg"), lax.axis_index("sub")
    n_up, width = up.shape[0], up.shape[2]
    slots = ops.shape[0]
    rows = leaf.shape[1] // n_up
    n_high = n_sub // 2
    side, core, high = seg % 2, sub % 2, sub // 2
    partner = seg + 1 - 2 * side
    other_side = 1 - side
    sibling = sub + 1 - 2 * core
    target = seg + 2 - 4 * side
    origin = seg - 2 + 4 * side
    has_target = (target >= 0) & (target < n_seg)
    has_origin = (origin >= 0) & (origin < n_seg)
    tiles = width // LANES
    half = rows // PARTS
    group_rows = rows * n_sub
    empty_row = 3 * group_rows

    leaf_copies = [
        pltpu.make_async_copy(leaf_hbm.at[:, pl.ds(t * LANES, LANES)], leaf.at[t], leaf_sem.at[t])
        for t in range(tiles)
    ]
    for c in leaf_copies:
        c.start()
    up_copies = [pltpu.make_async_copy(up_hbm.at[c], up.at[c], up_sem.at[c]) for c in range(n_up)]
    for c in up_copies:
        c.start()
    middle = slots // 2
    ops_copies = [
        pltpu.make_async_copy(ops_hbm.at[at], ops.at[at], ops_sem.at[k])
        for k, at in enumerate((pl.ds(0, middle), pl.ds(middle, slots - middle)))
    ]

    barrier = pltpu.get_barrier_semaphore()

    def greet(to_seg, to_sub):
        pl.semaphore_signal(barrier, inc=1, device_id=(to_seg, to_sub), device_id_type=MESH)

    def peer(step):
        return lax.rem(high + step, n_high) * 2 + core

    greet(seg, sibling)
    greet(partner, sub)
    for step in range(1, n_high):
        greet(seg, peer(step))

    @pl.when(has_target)
    def _():
        greet(target, sub)

    @pl.when(has_origin)
    def _():
        greet(origin, sub)

    box[pl.ds(empty_row * tiles, 8 * tiles), :] = jnp.zeros((8 * tiles, LANES), jnp.float32)

    for c in leaf_copies:
        c.wait()
    total = jnp.zeros((rows, width), jnp.float32)
    for c in range(n_up):
        up_copies[c].wait()
        if c == n_up // 2:
            for one in ops_copies:
                one.start()
        child = jnp.concatenate(
            [leaf[t, pl.ds(c, rows, stride=n_up), :] for t in range(tiles)], axis=1
        )
        first, second = split(child)
        up_first, up_second = split(up[c])
        both = jnp.concatenate([first, second], axis=0)
        out = jnp.dot(both, up_first, preferred_element_type=jnp.float32)
        total = total + (out[:rows] + out[rows:])
        total = total + jnp.dot(first, up_second, preferred_element_type=jnp.float32)
    own_start = pl.multiple_of((side * n_sub + sub) * rows * tiles, 8)
    for t in range(tiles):
        box[pl.ds(own_start + t, rows, stride=tiles), :] = total[:, t * LANES : (t + 1) * LANES]

    pl.semaphore_wait(barrier, 1 + n_high + has_target.astype(jnp.int32) + has_origin.astype(jnp.int32))

    names = {}

    def copy(name, src, dst, to_seg, to_sub):
        k = names.setdefault(name, len(names))
        return pltpu.make_async_remote_copy(
            src_ref=src, dst_ref=dst, send_sem=send_sem.at[k], recv_sem=recv_sem.at[k],
            device_id=(to_seg, to_sub), device_id_type=MESH,
        )

    def place(group, k, part=None):
        start = (group * n_sub + k) * rows * tiles
        if part is None:
            return box.at[pl.ds(pl.multiple_of(start, 8), rows * tiles)]
        return box.at[pl.ds(pl.multiple_of(start + part * half * tiles, 8), half * tiles)]

    sent = []

    def go(c):
        c.start()
        sent.append(c)
        return c

    def to_x(part):
        at = place(side, sub, part)
        return copy(("x", part), at, at, partner, sub)

    def from_x(part):
        at = place(other_side, sub, part)
        return copy(("x", part), at, at, partner, sub)

    def to_y(step, part):
        at = place(side, sub, part)
        return copy(("y", step, part), at, at, seg, peer(step))

    def from_y(step, part):
        at = place(side, peer(n_high - step), part)
        return copy(("y", step, part), at, at, seg, peer(step))

    def xy(step, part):
        at = place(other_side, sub, part)
        return copy(("xy", step, part), at, at, seg, peer(step))

    def from_xy(step, part):
        at = place(other_side, peer(n_high - step), part)
        return copy(("xy", step, part), at, at, seg, peer(step))

    def yx(step, part):
        at = place(side, peer(step), part)
        return copy(("yx", step, part), at, at, partner, sub)

    def from_yx(step, part):
        at = place(other_side, peer(step), part)
        return copy(("yx", step, part), at, at, partner, sub)

    def z(step, part):
        return copy(
            ("z", step, part), place(other_side, peer(step), part), place(2, peer(step), part), target, sub
        )

    def to_sibling(step, which):
        at = place((side, other_side, 2)[which], peer(step))
        return copy(("s", step, which), at, at, seg, sibling)

    def from_sibling(step, which):
        s = lax.rem(high + step, n_high) * 2 + 1 - core
        at = place((side, other_side, 2)[which], s)
        return copy(("s", step, which), at, at, seg, sibling)

    for part in range(PARTS):
        go(to_x(part))
        for step in range(1, n_high):
            go(to_y(step, PARTS - 1 - part))
    go(to_sibling(0, 0))

    def split_ops(start, stop):
        @pl.loop(start, stop)
        def _(j):
            ops_high[j], ops_low[j] = split(ops[j])

    ops_copies[0].wait()
    split_ops(0, middle)

    for part in range(PARTS):
        from_x(part).wait_recv()

        @pl.when(has_target)
        def _():
            z(0, part).start()

        for step in range(1, n_high):
            if part < PARTS // 2:
                go(xy(step, part))
        for step in range(1, n_high):
            from_y(step, PARTS - 1 - part).wait_recv()
            if part < PARTS // 2:
                go(yx(n_high - step, PARTS - 1 - part))

    go(to_sibling(0, 1))
    for step in range(1, n_high):
        go(to_sibling(n_high - step, 0))

    for part in range(PARTS // 2):
        for step in range(1, n_high):
            from_xy(step, part).wait_recv()

            @pl.when(has_target)
            def _():
                z(n_high - step, part).start()

            from_yx(step, PARTS - 1 - part).wait_recv()

            @pl.when(has_target)
            def _():
                z(step, PARTS - 1 - part).start()

    for step in range(1, n_high):
        go(to_sibling(step, 1))

    ops_copies[1].wait()
    split_ops(middle, slots)

    for step in range(n_high):
        from_sibling(step, 0).wait_recv()

    for step in range(n_high):
        from_sibling(step, 1).wait_recv()

    @pl.when(has_origin)
    def _():
        for step in range(n_high):
            for part in range(PARTS):
                z(step, part).wait_recv()
            to_sibling(step, 2).start()
        for step in range(n_high):
            from_sibling(step, 2).wait_recv()

    for c in sent:
        c.wait_send()

    @pl.when(has_target)
    def _():
        for step in range(n_high):
            for part in range(PARTS):
                z(step, part).wait_send()

    @pl.when(has_origin)
    def _():
        for step in range(n_high):
            to_sibling(step, 2).wait_send()


def combine(
    n_sub, src_t, owner, box, ops_high, ops_low, parent_out, owned_out, local_out,
    where_v, where_s, first_rows, second_rows, where_sem,
):
    seg, sub = lax.axis_index("seg"), lax.axis_index("sub")
    rows, width = local_out.shape
    slots = src_t.shape[0]
    tiles = width // LANES
    side = seg % 2
    group_rows = rows * n_sub
    empty_row = 3 * group_rows
    batches = slots // BATCH

    pair_start = (seg - side) * group_rows
    table = jnp.concatenate([src_t[...], jnp.broadcast_to(owner[...], (8, rows))], axis=0)
    local = table - pair_start
    local = jnp.where(local < 0, local + 3 * group_rows, local)
    local = jnp.where(table < 0, empty_row, jnp.clip(local, 0, empty_row))
    where_v[...] = local * tiles
    where_copy = pltpu.make_async_copy(where_v, where_s, where_sem.at[0])
    where_copy.start()

    def spread(ref, start):
        return jnp.concatenate(
            [ref[pl.ds(start + t, rows, stride=tiles), :] for t in range(tiles)], axis=1
        )

    def gather(into, slot, count):
        for i in range(count):
            for r in range(rows):
                at = pl.ds(pl.multiple_of(where_s[slot + i, r], tiles), tiles)
                into[pl.ds((i * rows + r) * tiles, tiles), :] = box[at, :]

    parent_out[...] = spread(box, pl.multiple_of((side * n_sub + sub) * rows * tiles, 8))
    where_copy.wait()
    gather(second_rows, slots, 1)
    owned_out[...] = spread(second_rows, 0)
    gather(first_rows, 0, BATCH)
    local_out[...] = jnp.zeros((rows, width), jnp.float32)

    def translate(rows_of, slot):
        parts = [split(spread(rows_of, i * rows * tiles)) for i in range(BATCH)]
        first = jnp.concatenate([p[0] for p in parts], axis=1)
        second = jnp.concatenate([p[1] for p in parts], axis=1)
        both = jnp.concatenate([first, second], axis=0)
        ops_first = ops_high[pl.ds(slot, BATCH)].reshape(BATCH * width, width)
        ops_second = ops_low[pl.ds(slot, BATCH)].reshape(BATCH * width, width)
        out = jnp.dot(both, ops_first, preferred_element_type=jnp.float32)
        rest = jnp.dot(first, ops_second, preferred_element_type=jnp.float32)
        local_out[...] += out[:rows] + (out[rows:] + rest)

    @pl.loop(0, batches // 2 - 1)
    def _(b):
        slot = b * (2 * BATCH)
        gather(second_rows, slot + BATCH, BATCH)
        translate(first_rows, slot)
        gather(first_rows, slot + 2 * BATCH, BATCH)
        translate(second_rows, slot + BATCH)

    gather(second_rows, slots - BATCH, BATCH)
    translate(first_rows, slots - 2 * BATCH)
    translate(second_rows, slots - BATCH)


def on_device(n_seg, n_sub, leaf_mult, m2m_ops, m2l_ops, owner_box, src_list):
    rows, width = leaf_mult.shape[0] // 8, leaf_mult.shape[1]
    slots = src_list.shape[1]
    n_high = n_sub // 2
    messages = PARTS * (3 * n_high - 1) + 3 * n_high
    group_rows = rows * n_sub
    tiles = width // LANES
    vmem = pl.BlockSpec(memory_space=pltpu.VMEM)
    hbm = pl.BlockSpec(memory_space=pl.ANY)
    half_ops = jax.ShapeDtypeStruct(m2l_ops.shape, jnp.bfloat16)
    box, ops_high, ops_low = pl.pallas_call(
        functools.partial(exchange, n_seg, n_sub),
        out_shape=(
            jax.ShapeDtypeStruct(((3 * group_rows + 8) * tiles, LANES), jnp.float32), half_ops, half_ops
        ),
        in_specs=[hbm, hbm, hbm],
        out_specs=(vmem, vmem, vmem),
        scratch_shapes=[
            pltpu.VMEM((tiles, leaf_mult.shape[0], LANES), jnp.float32),
            pltpu.VMEM(m2m_ops.shape, jnp.float32),
            pltpu.VMEM(m2l_ops.shape, jnp.float32),
            pltpu.SemaphoreType.DMA((2,)),
            pltpu.SemaphoreType.DMA((tiles,)),
            pltpu.SemaphoreType.DMA((m2m_ops.shape[0],)),
            pltpu.SemaphoreType.DMA((messages,)),
            pltpu.SemaphoreType.DMA((messages,)),
        ],
        compiler_params=pltpu.CompilerParams(
            collective_id=0, has_side_effects=True, vmem_limit_bytes=EXCHANGE_VMEM
        ),
    )(*(pltpu.with_memory_space_constraint(a, pltpu.HBM) for a in (leaf_mult, m2m_ops, m2l_ops)))
    out = jax.ShapeDtypeStruct((rows, width), jnp.float32)
    return pl.pallas_call(
        functools.partial(combine, n_sub),
        out_shape=(out, out, out),
        in_specs=[vmem] * 5,
        out_specs=(vmem, vmem, vmem),
        scratch_shapes=[
            pltpu.VMEM((slots + 8, rows), jnp.int32),
            pltpu.SMEM((slots + 8, rows), jnp.int32),
            pltpu.VMEM((BATCH * rows * tiles, LANES), jnp.float32),
            pltpu.VMEM((BATCH * rows * tiles, LANES), jnp.float32),
            pltpu.SemaphoreType.DMA((1,)),
        ],
        compiler_params=pltpu.CompilerParams(vmem_limit_bytes=COMBINE_VMEM),
    )(src_list.T, owner_box.reshape(1, rows), box, ops_high, ops_low)


def solution(mesh):
    n_seg, n_sub = mesh.shape["seg"], mesh.shape["sub"]
    in_specs = (P(("seg", "sub"), None), P(), P(), P(("seg", "sub")), P(("seg", "sub"), None))
    out_specs = (P(("seg", "sub"), None), P(("seg", "sub"), None), P(("seg", "sub"), None))
    return jax.shard_map(
        functools.partial(on_device, n_seg, n_sub),
        mesh=mesh, in_specs=in_specs, out_specs=out_specs, check_vma=False,
    )
```

time: 29.2 us -> 23.7 us (0.81)
  the two profiles are of different devices: /device:TPU:17 before, /device:TPU:11 now
where the time goes in v1:
time: 23.7 us; the launch traced here: 23.5 us
  Pallas kernels  22.9 us (97%)
  between operations  0.67 us (3%)
    pallas_call x1, Pallas kernels, on_device(): pl.pallas_call(functools.partial(exchange, n_seg, n_sub), out_shape=(jax....  16.7 us
    pallas_call x1, Pallas kernels, on_device(): pl.pallas_call(functools.partial(combine, n_sub), out_shape=(out, out, ou...  6.21 us

profile of v1, /device:TPU:11, one launch (start us, length us, event | category | flops | bytes accessed | tf_op | source)
XLA Modules:
  0.0 23.5 jit_solution(13859494783277211398)
XLA Ops:
  0.6 0.0 copy-start
  0.6 0.0 copy-start.1
  0.7 16.7 %shard_map.76 = (f32[3088,128]{1,0:T(8,128)S(1)}, bf16[32,256,256]{2,1,0:T(8,128)(2,1)S(1)}, bf16[32,256,256]{2,1,0:T(8,128)(2,1)S(1)}) custom-call(f32[1024,256]{1,0:T(8,128)} %leaf_hbm.1, f32[8,256,256]{2,1,0:T(8,128)} %up_hbm.1, f32[32,256,256]{2,1,0:T(8,128)} %ops_hbm.1), custom_call_target="tpu_custom_call" | custom-call | tf_op jit(solution)/shard_map/pallas_call | solution.py:332
  17.3 0.0 copy-done
  17.3 0.0 copy-done.1
  17.3 6.2 %shard_map.77 = (f32[128,256]{1,0:T(8,128)}, f32[128,256]{1,0:T(8,128)}, f32[128,256]{1,0:T(8,128)}) custom-call(s32[32,128]{1,0:T(8,128)S(1)} %bitcast.2, s32[1,128]{1,0:T(1,128)S(1)} %bitcast.3, f32[3088,128]{1,0:T(8,128)S(1)} %get-tuple-element.6.box, bf16[32,256,256]{2,1,0:T(8,128)(2,1)S(1)} %get-tuple-element.7.ops_high, ...), custom_call_target="tpu_custom_call" | custom-call | tf_op jit(solution)/shard_map/pallas_call | solution.py:354
Async XLA Ops:
  0.6 16.7 %copy-start = (s32[128,32]{0,1:T(8,128)S(1)}, s32[128,32]{0,1:T(8,128)}, u32[]{:S(2)}) copy-start(s32[128,32]{0,1:T(8,128)} %param.9) | copy-start | bytes 49156
  0.6 16.7 %copy-start.1 = (s32[128]{0:T(128)S(1)}, s32[128]{0:T(128)}, u32[]{:S(2)}) copy-start(s32[128]{0:T(128)} %param.8) | copy-start | bytes 1540

commit v2 on v1

--- a/solution.py
+++ b/solution.py
@@ -306,17 +306,13 @@
         rest = jnp.dot(first, ops_second, preferred_element_type=jnp.float32)
         local_out[...] += out[:rows] + (out[rows:] + rest)
 
-    @pl.loop(0, batches // 2 - 1)
-    def _(b):
-        slot = b * (2 * BATCH)
+    for b in range(0, batches, 2):
+        slot = b * BATCH
         gather(second_rows, slot + BATCH, BATCH)
         translate(first_rows, slot)
-        gather(first_rows, slot + 2 * BATCH, BATCH)
+        if b + 2 < batches:
+            gather(first_rows, slot + 2 * BATCH, BATCH)
         translate(second_rows, slot + BATCH)
-
-    gather(second_rows, slots - BATCH, BATCH)
-    translate(first_rows, slots - 2 * BATCH)
-    translate(second_rows, slots - BATCH)
 
 
 def on_device(n_seg, n_sub, leaf_mult, m2m_ops, m2l_ops, owner_box, src_list):

time: 23.7 us -> 23 us (0.970)
  Pallas kernels: 22.9 us -> 22.1 us
    pallas_call x1, Pallas kernels: 6.21 us -> 5.48 us  [on_device(): pl.pallas_call(functools.partial(combine, n_sub), out_shape=(out, out, ou...]
where the time goes in v2:
time: 23 us; the launch traced here: 22.8 us
  Pallas kernels  22.1 us (96%)
  between operations  0.67 us (3%)
    pallas_call x1, Pallas kernels, on_device(): pl.pallas_call(functools.partial(exchange, n_seg, n_sub), out_shape=(jax....  16.7 us
    pallas_call x1, Pallas kernels, on_device(): pl.pallas_call(functools.partial(combine, n_sub), out_shape=(out, out, ou...  5.48 us

profile of v2, /device:TPU:11, one launch (start us, length us, event | category | flops | bytes accessed | tf_op | source)
XLA Modules:
  0.0 22.8 jit_solution(4318763506201239111)
XLA Ops:
  0.6 0.0 copy-start
  0.6 0.0 copy-start.1
  0.7 16.7 %shard_map.76 = (f32[3088,128]{1,0:T(8,128)S(1)}, bf16[32,256,256]{2,1,0:T(8,128)(2,1)S(1)}, bf16[32,256,256]{2,1,0:T(8,128)(2,1)S(1)}) custom-call(f32[1024,256]{1,0:T(8,128)} %leaf_hbm.1, f32[8,256,256]{2,1,0:T(8,128)} %up_hbm.1, f32[32,256,256]{2,1,0:T(8,128)} %ops_hbm.1), custom_call_target="tpu_custom_call" | custom-call | tf_op jit(solution)/shard_map/pallas_call | solution.py:328
  17.3 0.0 copy-done
  17.3 0.0 copy-done.1
  17.3 5.5 %shard_map.77 = (f32[128,256]{1,0:T(8,128)}, f32[128,256]{1,0:T(8,128)}, f32[128,256]{1,0:T(8,128)}) custom-call(s32[32,128]{1,0:T(8,128)S(1)} %bitcast.2, s32[1,128]{1,0:T(1,128)S(1)} %bitcast.3, f32[3088,128]{1,0:T(8,128)S(1)} %get-tuple-element.6.box, bf16[32,256,256]{2,1,0:T(8,128)(2,1)S(1)} %get-tuple-element.7.ops_high, ...), custom_call_target="tpu_custom_call" | custom-call | tf_op jit(solution)/shard_map/pallas_call | solution.py:350
Async XLA Ops:
  0.6 16.7 %copy-start = (s32[128,32]{0,1:T(8,128)S(1)}, s32[128,32]{0,1:T(8,128)}, u32[]{:S(2)}) copy-start(s32[128,32]{0,1:T(8,128)} %param.9) | copy-start | bytes 49156
  0.6 16.7 %copy-start.1 = (s32[128]{0:T(128)S(1)}, s32[128]{0:T(128)}, u32[]{:S(2)}) copy-start(s32[128]{0:T(128)} %param.8) | copy-start | bytes 1540

commit v3 on v2

--- a/solution.py
+++ b/solution.py
@@ -11,6 +11,8 @@
 LANES = 128
 BATCH = 4
 PARTS = 4
+DIRECT = 1
+CROSS = 1
 EXCHANGE_VMEM = 24 << 20
 COMBINE_VMEM = 16 << 20
 
@@ -23,7 +25,7 @@
 
 def exchange(
     n_seg, n_sub, leaf_hbm, up_hbm, ops_hbm, box, ops_high, ops_low,
-    leaf, up, ops, ops_sem, leaf_sem, up_sem, send_sem, recv_sem,
+    leaf, up, ops, relay, ops_sem, leaf_sem, up_sem, send_sem, recv_sem,
 ):
     seg, sub = lax.axis_index("seg"), lax.axis_index("sub")
     n_up, width = up.shape[0], up.shape[2]
@@ -74,10 +76,14 @@
     @pl.when(has_target)
     def _():
         greet(target, sub)
+        for step in range(1, n_high):
+            greet(target, peer(step))
 
     @pl.when(has_origin)
     def _():
         greet(origin, sub)
+        for step in range(1, n_high):
+            greet(origin, peer(step))
 
     box[pl.ds(empty_row * tiles, 8 * tiles), :] = jnp.zeros((8 * tiles, LANES), jnp.float32)
 
@@ -102,7 +108,9 @@
     for t in range(tiles):
         box[pl.ds(own_start + t, rows, stride=tiles), :] = total[:, t * LANES : (t + 1) * LANES]
 
-    pl.semaphore_wait(barrier, 1 + n_high + has_target.astype(jnp.int32) + has_origin.astype(jnp.int32))
+    pl.semaphore_wait(
+        barrier, 1 + n_high + n_high * (has_target.astype(jnp.int32) + has_origin.astype(jnp.int32))
+    )
 
     names = {}
 
@@ -121,10 +129,12 @@
 
     sent = []
 
-    def go(c):
-        c.start()
-        sent.append(c)
-        return c
+    def go(c, when=None):
+        sent.append((c, when))
+        if when is None:
+            c.start()
+        else:
+            pl.when(when)(c.start)
 
     def to_x(part):
         at = place(side, sub, part)
@@ -142,6 +152,12 @@
         at = place(side, peer(n_high - step), part)
         return copy(("y", step, part), at, at, seg, peer(step))
 
+    def over_z(part):
+        return copy(("o", part), place(side, sub, part), relay.at[part], origin, sub)
+
+    def over_x(part):
+        return copy(("ox", part), relay.at[part], place(2, sub, part), partner, sub)
+
     def xy(step, part):
         at = place(other_side, sub, part)
         return copy(("xy", step, part), at, at, seg, peer(step))
@@ -158,24 +174,37 @@
         at = place(other_side, peer(step), part)
         return copy(("yx", step, part), at, at, partner, sub)
 
-    def z(step, part):
+    def z(part):
+        return copy(("z", part), place(other_side, sub, part), place(2, sub, part), target, sub)
+
+    def yz(step, part):
         return copy(
-            ("z", step, part), place(other_side, peer(step), part), place(2, peer(step), part), target, sub
+            ("yz", step, part), place(other_side, sub, part), place(2, sub, part), target, peer(step)
         )
 
-    def to_sibling(step, which):
-        at = place((side, other_side, 2)[which], peer(step))
-        return copy(("s", step, which), at, at, seg, sibling)
-
-    def from_sibling(step, which):
-        s = lax.rem(high + step, n_high) * 2 + 1 - core
-        at = place((side, other_side, 2)[which], s)
-        return copy(("s", step, which), at, at, seg, sibling)
-
-    for part in range(PARTS):
-        go(to_x(part))
-        for step in range(1, n_high):
-            go(to_y(step, PARTS - 1 - part))
+    def from_yz(step, part):
+        at = place(2, peer(n_high - step), part)
+        return copy(("yz", step, part), at, at, target, peer(step))
+
+    def to_sibling(group, step, part=None):
+        at = place((side, other_side, 2)[group], peer(step), part)
+        return copy(("s", group, step, part), at, at, seg, sibling)
+
+    def from_sibling(group, step, part=None):
+        theirs = lax.rem(high + step, n_high) * 2 + 1 - core
+        at = place((side, other_side, 2)[group], theirs, part)
+        return copy(("s", group, step, part), at, at, seg, sibling)
+
+    parts = list(range(PARTS))
+    through_x, through_z = parts[DIRECT:], parts[:DIRECT]
+    y_order = parts[CROSS:] + parts[:CROSS]
+
+    for i in parts:
+        go(to_x(i))
+        for step in range(1, n_high):
+            go(to_y(step, y_order[i]))
+        if i < len(through_x):
+            go(over_z(through_x[i]), has_origin)
     go(to_sibling(0, 0))
 
     def split_ops(start, stop):
@@ -186,73 +215,62 @@
     ops_copies[0].wait()
     split_ops(0, middle)
 
-    for part in range(PARTS):
-        from_x(part).wait_recv()
-
-        @pl.when(has_target)
-        def _():
-            z(0, part).start()
-
-        for step in range(1, n_high):
-            if part < PARTS // 2:
-                go(xy(step, part))
-        for step in range(1, n_high):
-            from_y(step, PARTS - 1 - part).wait_recv()
-            if part < PARTS // 2:
-                go(yx(n_high - step, PARTS - 1 - part))
-
-    go(to_sibling(0, 1))
+    for i in parts:
+        from_x(i).wait_recv()
+        for step in range(1, n_high):
+            go(yz(step, i), has_target)
+        if i in through_z:
+            go(z(i), has_target)
+        for step in range(1, n_high):
+            if i < CROSS:
+                go(xy(step, i))
+        if i < len(through_x):
+            pl.when(has_target)(over_z(through_x[i]).wait_recv)
+            go(over_x(through_x[i]), has_target)
+        for step in range(1, n_high):
+            from_y(step, y_order[i]).wait_recv()
+            if y_order[i] >= CROSS:
+                go(yx(n_high - step, y_order[i]))
+
+    go(to_sibling(1, 0))
     for step in range(1, n_high):
-        go(to_sibling(n_high - step, 0))
-
-    for part in range(PARTS // 2):
-        for step in range(1, n_high):
-            from_xy(step, part).wait_recv()
-
-            @pl.when(has_target)
-            def _():
-                z(n_high - step, part).start()
-
-            from_yx(step, PARTS - 1 - part).wait_recv()
-
-            @pl.when(has_target)
-            def _():
-                z(step, PARTS - 1 - part).start()
-
-    for step in range(1, n_high):
-        go(to_sibling(step, 1))
+        go(to_sibling(0, n_high - step))
 
     ops_copies[1].wait()
     split_ops(middle, slots)
 
+    for i in parts:
+        one = z(i) if i in through_z else over_x(i)
+        pl.when(has_origin)(one.wait_recv)
+        go(to_sibling(2, 0, i), has_origin)
+        for step in range(1, n_high):
+            if i < CROSS:
+                from_xy(step, i).wait_recv()
+                go(to_sibling(1, n_high - step, i))
+            else:
+                from_yx(step, i).wait_recv()
+                go(to_sibling(1, step, i))
+            pl.when(has_origin)(from_yz(step, i).wait_recv)
+            go(to_sibling(2, n_high - step, i), has_origin)
+
     for step in range(n_high):
-        from_sibling(step, 0).wait_recv()
-
-    for step in range(n_high):
-        from_sibling(step, 1).wait_recv()
+        from_sibling(0, step).wait_recv()
+    from_sibling(1, 0).wait_recv()
+    for step in range(1, n_high):
+        for i in parts:
+            from_sibling(1, step, i).wait_recv()
 
     @pl.when(has_origin)
     def _():
         for step in range(n_high):
-            for part in range(PARTS):
-                z(step, part).wait_recv()
-            to_sibling(step, 2).start()
-        for step in range(n_high):
-            from_sibling(step, 2).wait_recv()
-
-    for c in sent:
-        c.wait_send()
-
-    @pl.when(has_target)
-    def _():
-        for step in range(n_high):
-            for part in range(PARTS):
-                z(step, part).wait_send()
-
-    @pl.when(has_origin)
-    def _():
-        for step in range(n_high):
-            to_sibling(step, 2).wait_send()
+            for i in parts:
+                from_sibling(2, step, i).wait_recv()
+
+    for c, when in sent:
+        if when is None:
+            c.wait_send()
+        else:
+            pl.when(when)(c.wait_send)
 
 
 def combine(
@@ -319,7 +337,7 @@
     rows, width = leaf_mult.shape[0] // 8, leaf_mult.shape[1]
     slots = src_list.shape[1]
     n_high = n_sub // 2
-    messages = PARTS * (3 * n_high - 1) + 3 * n_high
+    messages = PARTS * (4 + 5 * (n_high - 1)) + 1 + n_high
     group_rows = rows * n_sub
     tiles = width // LANES
     vmem = pl.BlockSpec(memory_space=pltpu.VMEM)
@@ -336,6 +354,7 @@
             pltpu.VMEM((tiles, leaf_mult.shape[0], LANES), jnp.float32),
             pltpu.VMEM(m2m_ops.shape, jnp.float32),
             pltpu.VMEM(m2l_ops.shape, jnp.float32),
+            pltpu.VMEM((PARTS, rows // PARTS * tiles, LANES), jnp.float32),
             pltpu.SemaphoreType.DMA((2,)),
             pltpu.SemaphoreType.DMA((tiles,)),
             pltpu.SemaphoreType.DMA((m2m_ops.shape[0],)),

time: 23 us -> 21.4 us (0.930)
  the two profiles are of different devices: /device:TPU:11 before, /device:TPU:17 now
where the time goes in v3:
time: 21.4 us; the launch traced here: 21.2 us
  Pallas kernels  20.5 us (96%)
  between operations  0.67 us (3%)
    pallas_call x1, Pallas kernels, on_device(): pl.pallas_call(functools.partial(exchange, n_seg, n_sub), out_shape=(jax....  15 us
    pallas_call x1, Pallas kernels, on_device(): pl.pallas_call(functools.partial(combine, n_sub), out_shape=(out, out, ou...  5.47 us

profile of v3, /device:TPU:17, one launch (start us, length us, event | category | flops | bytes accessed | tf_op | source)
XLA Modules:
  0.0 21.2 jit_solution(18409217768782637591)
XLA Ops:
  0.6 0.0 copy-start
  0.6 0.0 copy-start.1
  0.7 15.0 %shard_map.76 = (f32[3088,128]{1,0:T(8,128)S(1)}, bf16[32,256,256]{2,1,0:T(8,128)(2,1)S(1)}, bf16[32,256,256]{2,1,0:T(8,128)(2,1)S(1)}) custom-call(f32[1024,256]{1,0:T(8,128)} %leaf_hbm.1, f32[8,256,256]{2,1,0:T(8,128)} %up_hbm.1, f32[32,256,256]{2,1,0:T(8,128)} %ops_hbm.1), custom_call_target="tpu_custom_call" | custom-call | tf_op jit(solution)/shard_map/pallas_call | solution.py:346
  15.7 0.0 copy-done
  15.7 0.0 copy-done.1
  15.7 5.5 %shard_map.77 = (f32[128,256]{1,0:T(8,128)}, f32[128,256]{1,0:T(8,128)}, f32[128,256]{1,0:T(8,128)}) custom-call(s32[32,128]{1,0:T(8,128)S(1)} %bitcast.2, s32[1,128]{1,0:T(1,128)S(1)} %bitcast.3, f32[3088,128]{1,0:T(8,128)S(1)} %get-tuple-element.6.box, bf16[32,256,256]{2,1,0:T(8,128)(2,1)S(1)} %get-tuple-element.7.ops_high, ...), custom_call_target="tpu_custom_call" | custom-call | tf_op jit(solution)/shard_map/pallas_call | solution.py:369
Async XLA Ops:
  0.6 15.1 %copy-start = (s32[128,32]{0,1:T(8,128)S(1)}, s32[128,32]{0,1:T(8,128)}, u32[]{:S(2)}) copy-start(s32[128,32]{0,1:T(8,128)} %param.9) | copy-start | bytes 49156
  0.6 15.1 %copy-start.1 = (s32[128]{0:T(128)S(1)}, s32[128]{0:T(128)}, u32[]{:S(2)}) copy-start(s32[128]{0:T(128)} %param.8) | copy-start | bytes 1540

commit v4 on v3

--- a/solution.py
+++ b/solution.py
@@ -13,6 +13,7 @@
 PARTS = 4
 DIRECT = 1
 CROSS = 1
+CHILDREN = 4
 EXCHANGE_VMEM = 24 << 20
 COMBINE_VMEM = 16 << 20
 
@@ -51,9 +52,6 @@
     ]
     for c in leaf_copies:
         c.start()
-    up_copies = [pltpu.make_async_copy(up_hbm.at[c], up.at[c], up_sem.at[c]) for c in range(n_up)]
-    for c in up_copies:
-        c.start()
     middle = slots // 2
     ops_copies = [
         pltpu.make_async_copy(ops_hbm.at[at], ops.at[at], ops_sem.at[k])
@@ -85,25 +83,39 @@
         for step in range(1, n_high):
             greet(origin, peer(step))
 
+    up_copies = [
+        pltpu.make_async_copy(
+            up_hbm.at[pl.ds(c, CHILDREN)], up.at[pl.ds(c, CHILDREN)], up_sem.at[c // CHILDREN]
+        )
+        for c in range(0, n_up, CHILDREN)
+    ]
+    for c in up_copies:
+        c.start()
+
     box[pl.ds(empty_row * tiles, 8 * tiles), :] = jnp.zeros((8 * tiles, LANES), jnp.float32)
 
     for c in leaf_copies:
         c.wait()
-    total = jnp.zeros((rows, width), jnp.float32)
-    for c in range(n_up):
-        up_copies[c].wait()
-        if c == n_up // 2:
-            for one in ops_copies:
-                one.start()
+    total = None
+    for k, one in enumerate(up_copies):
+        one.wait()
+        if k == len(up_copies) - 1:
+            for c in ops_copies:
+                c.start()
         child = jnp.concatenate(
-            [leaf[t, pl.ds(c, rows, stride=n_up), :] for t in range(tiles)], axis=1
+            [
+                leaf[t, pl.ds(k * CHILDREN + c, rows, stride=n_up), :]
+                for c in range(CHILDREN) for t in range(tiles)
+            ],
+            axis=1,
         )
         first, second = split(child)
-        up_first, up_second = split(up[c])
+        up_first, up_second = split(up[pl.ds(k * CHILDREN, CHILDREN)].reshape(CHILDREN * width, width))
         both = jnp.concatenate([first, second], axis=0)
         out = jnp.dot(both, up_first, preferred_element_type=jnp.float32)
-        total = total + (out[:rows] + out[rows:])
-        total = total + jnp.dot(first, up_second, preferred_element_type=jnp.float32)
+        rest = jnp.dot(first, up_second, preferred_element_type=jnp.float32)
+        term = out[:rows] + (out[rows:] + rest)
+        total = term if total is None else total + term
     own_start = pl.multiple_of((side * n_sub + sub) * rows * tiles, 8)
     for t in range(tiles):
         box[pl.ds(own_start + t, rows, stride=tiles), :] = total[:, t * LANES : (t + 1) * LANES]

time: 21.4 us -> 20.3 us (0.949)
  Pallas kernels: 20.5 us -> 19.5 us
    pallas_call x1, Pallas kernels: 15 us -> 14 us  [on_device(): pl.pallas_call(functools.partial(exchange, n_seg, n_sub), out_shape=(jax....]
where the time goes in v4:
time: 20.3 us; the launch traced here: 20.2 us
  Pallas kernels  19.5 us (96%)
  between operations  0.67 us (3%)
    pallas_call x1, Pallas kernels, on_device(): pl.pallas_call(functools.partial(exchange, n_seg, n_sub), out_shape=(jax....  14 us
    pallas_call x1, Pallas kernels, on_device(): pl.pallas_call(functools.partial(combine, n_sub), out_shape=(out, out, ou...  5.48 us

profile of v4, /device:TPU:17, one launch (start us, length us, event | category | flops | bytes accessed | tf_op | source)
XLA Modules:
  0.0 20.2 jit_solution(13229633559201289969)
XLA Ops:
  0.6 0.0 copy-start
  0.6 0.0 copy-start.1
  0.7 14.0 %shard_map.76 = (f32[3088,128]{1,0:T(8,128)S(1)}, bf16[32,256,256]{2,1,0:T(8,128)(2,1)S(1)}, bf16[32,256,256]{2,1,0:T(8,128)(2,1)S(1)}) custom-call(f32[1024,256]{1,0:T(8,128)} %leaf_hbm.1, f32[8,256,256]{2,1,0:T(8,128)} %up_hbm.1, f32[32,256,256]{2,1,0:T(8,128)} %ops_hbm.1), custom_call_target="tpu_custom_call" | custom-call | tf_op jit(solution)/shard_map/pallas_call | solution.py:358
  14.7 0.0 copy-done
  14.7 0.0 copy-done.1
  14.7 5.5 %shard_map.77 = (f32[128,256]{1,0:T(8,128)}, f32[128,256]{1,0:T(8,128)}, f32[128,256]{1,0:T(8,128)}) custom-call(s32[32,128]{1,0:T(8,128)S(1)} %bitcast.2, s32[1,128]{1,0:T(1,128)S(1)} %bitcast.3, f32[3088,128]{1,0:T(8,128)S(1)} %get-tuple-element.6.box, bf16[32,256,256]{2,1,0:T(8,128)(2,1)S(1)} %get-tuple-element.7.ops_high, ...), custom_call_target="tpu_custom_call" | custom-call | tf_op jit(solution)/shard_map/pallas_call | solution.py:381
Async XLA Ops:
  0.6 14.0 %copy-start = (s32[128,32]{0,1:T(8,128)S(1)}, s32[128,32]{0,1:T(8,128)}, u32[]{:S(2)}) copy-start(s32[128,32]{0,1:T(8,128)} %param.9) | copy-start | bytes 49156
  0.6 14.0 %copy-start.1 = (s32[128]{0:T(128)S(1)}, s32[128]{0:T(128)}, u32[]{:S(2)}) copy-start(s32[128]{0:T(128)} %param.8) | copy-start | bytes 1540

commit v5 on v4

--- a/solution.py
+++ b/solution.py
@@ -287,7 +287,7 @@
 
 def combine(
     n_sub, src_t, owner, box, ops_high, ops_low, parent_out, owned_out, local_out,
-    where_v, where_s, first_rows, second_rows, where_sem,
+    where_v, where_s, first_rows, second_rows, third_rows, where_sem,
 ):
     seg, sub = lax.axis_index("seg"), lax.axis_index("sub")
     rows, width = local_out.shape
@@ -304,8 +304,13 @@
     local = jnp.where(local < 0, local + 3 * group_rows, local)
     local = jnp.where(table < 0, empty_row, jnp.clip(local, 0, empty_row))
     where_v[...] = local * tiles
-    where_copy = pltpu.make_async_copy(where_v, where_s, where_sem.at[0])
-    where_copy.start()
+    early, late = pl.ds(0, 2 * BATCH), pl.ds(2 * BATCH, slots + 8 - 2 * BATCH)
+    where_copies = [
+        pltpu.make_async_copy(where_v.at[at], where_s.at[at], where_sem.at[k])
+        for k, at in enumerate((early, late))
+    ]
+    for c in where_copies:
+        c.start()
 
     def spread(ref, start):
         return jnp.concatenate(
@@ -319,10 +324,11 @@
                 into[pl.ds((i * rows + r) * tiles, tiles), :] = box[at, :]
 
     parent_out[...] = spread(box, pl.multiple_of((side * n_sub + sub) * rows * tiles, 8))
-    where_copy.wait()
-    gather(second_rows, slots, 1)
-    owned_out[...] = spread(second_rows, 0)
+    where_copies[0].wait()
     gather(first_rows, 0, BATCH)
+    where_copies[1].wait()
+    gather(third_rows, slots, 1)
+    owned_out[...] = spread(third_rows, 0)
     local_out[...] = jnp.zeros((rows, width), jnp.float32)
 
     def translate(rows_of, slot):
@@ -388,7 +394,8 @@
             pltpu.SMEM((slots + 8, rows), jnp.int32),
             pltpu.VMEM((BATCH * rows * tiles, LANES), jnp.float32),
             pltpu.VMEM((BATCH * rows * tiles, LANES), jnp.float32),
-            pltpu.SemaphoreType.DMA((1,)),
+            pltpu.VMEM((rows * tiles, LANES), jnp.float32),
+            pltpu.SemaphoreType.DMA((2,)),
         ],
         compiler_params=pltpu.CompilerParams(vmem_limit_bytes=COMBINE_VMEM),
     )(src_list.T, owner_box.reshape(1, rows), box, ops_high, ops_low)

time: 20.3 us -> 20 us (0.985)
  Pallas kernels: 19.5 us -> 19.2 us
    pallas_call x1, Pallas kernels: 5.48 us -> 5.17 us  [on_device(): pl.pallas_call(functools.partial(combine, n_sub), out_shape=(out, out, ou...]
where the time goes in v5:
time: 20 us; the launch traced here: 19.9 us
  Pallas kernels  19.2 us (96%)
  between operations  0.67 us (3%)
    pallas_call x1, Pallas kernels, on_device(): pl.pallas_call(functools.partial(exchange, n_seg, n_sub), out_shape=(jax....  14 us
    pallas_call x1, Pallas kernels, on_device(): pl.pallas_call(functools.partial(combine, n_sub), out_shape=(out, out, ou...  5.17 us

profile of v5, /device:TPU:17, one launch (start us, length us, event | category | flops | bytes accessed | tf_op | source)
XLA Modules:
  0.0 19.9 jit_solution(9658544973499430162)
XLA Ops:
  0.6 0.0 copy-start
  0.6 0.0 copy-start.1
  0.7 14.0 %shard_map.76 = (f32[3088,128]{1,0:T(8,128)S(1)}, bf16[32,256,256]{2,1,0:T(8,128)(2,1)S(1)}, bf16[32,256,256]{2,1,0:T(8,128)(2,1)S(1)}) custom-call(f32[1024,256]{1,0:T(8,128)} %leaf_hbm.1, f32[8,256,256]{2,1,0:T(8,128)} %up_hbm.1, f32[32,256,256]{2,1,0:T(8,128)} %ops_hbm.1), custom_call_target="tpu_custom_call" | custom-call | tf_op jit(solution)/shard_map/pallas_call | solution.py:364
  14.7 0.0 copy-done
  14.7 0.0 copy-done.1
  14.7 5.2 %shard_map.77 = (f32[128,256]{1,0:T(8,128)}, f32[128,256]{1,0:T(8,128)}, f32[128,256]{1,0:T(8,128)}) custom-call(s32[32,128]{1,0:T(8,128)S(1)} %bitcast.2, s32[1,128]{1,0:T(1,128)S(1)} %bitcast.3, f32[3088,128]{1,0:T(8,128)S(1)} %get-tuple-element.6.box, bf16[32,256,256]{2,1,0:T(8,128)(2,1)S(1)} %get-tuple-element.7.ops_high, ...), custom_call_target="tpu_custom_call" | custom-call | tf_op jit(solution)/shard_map/pallas_call | solution.py:387
Async XLA Ops:
  0.6 14.0 %copy-start = (s32[128,32]{0,1:T(8,128)S(1)}, s32[128,32]{0,1:T(8,128)}, u32[]{:S(2)}) copy-start(s32[128,32]{0,1:T(8,128)} %param.9) | copy-start | bytes 49156
  0.6 14.0 %copy-start.1 = (s32[128]{0:T(128)S(1)}, s32[128]{0:T(128)}, u32[]{:S(2)}) copy-start(s32[128]{0:T(128)} %param.8) | copy-start | bytes 1540
